TPU v7x, 32 devices: a whole 2x2x4 slice. The times are simulated.
32 devices in a mesh: groups: 2 (over x), band: 16 (over z, y, core).
Axes of the slice: x: 2, y: 2, z: 4, core: 2. Of those that a mesh axis runs over, the one named last changes fastest.
Arguments:
- orbitals: bfloat16 [2560, 32, 128], P(('groups', 'band')), parts along dimension 0, may hold values from -24 to 24
- potential: float32 [64, 128], P('groups'), parts along dimension 0, may hold values from -2 to 0
- plan: int32 [4, 16], P('groups'), parts along dimension 0, may hold values from 0 to 15, as said below
- owners: int32 [4, 16], P('groups'), parts along dimension 0, may hold values from 0 to 15, each once within a row
Outputs:
- filtered: bfloat16 [2560, 32, 128], P(('groups', 'band')), parts along dimension 0
- tiles: float32 [2, 2560, 80], P(None, ('groups', 'band')), parts along dimension 1
There are 2 independent parts, one for each index of `groups`. A program takes and returns all parts, laid end to end along the dimension named above; each array names one. Nothing has to cross between parts.
Inputs may be any that keep to these rules, and one draw needn't show every extreme that they name: In each of the 2 rounds the band groups are paired by a round-robin tournament: plan[r, i] is never i and plan[r, plan[r, i]] = i. `owners`: each row is a permutation of the band groups.
All inputs are finite; a program needn't handle non-finite values.
Results may differ from a plain program's by a relative error of at most 0.0055.
Values may be sent and summed in bfloat16 or wider, within the bound.
A program may use at most 192 MiB of HBM per device.

v0:
```python
import math
import jax
import jax.numpy as jnp
from jax import lax
from jax.sharding import PartitionSpec as P

NZ = 16
ROUNDS = 2
lower_edge = -2.5
cutoff_edge = 4.0
upper_edge = 8.5
half_width = (upper_edge - cutoff_edge) / 2.0
middle_point = (upper_edge + cutoff_edge) / 2.0


def with_halo(array, sides, width):
    for axis, dim in sides:
        devices, length = (lax.axis_size(axis), array.shape[dim])
        up = [(i, (i + 1) % devices) for i in range(devices - 1)]
        down = [(j, i) for i, j in up]
        last = lax.slice_in_dim(array, length - width, length, axis=dim)
        leading = lax.slice_in_dim(array, 0, width, axis=dim)
        before = lax.ppermute(last, axis, up)
        after = lax.ppermute(leading, axis, down)
        array = jnp.concatenate([before, array, after], axis=dim)
    return array


def chebyshev_filter(start_values, operator):
    sigma_zero = half_width / (lower_edge - middle_point)
    previous = start_values
    current = sigma_zero / half_width * (operator(start_values) - middle_point * start_values)
    sigma_now = sigma_zero
    sigma_next = 1.0 / (2.0 / sigma_zero - sigma_now)
    following = (
        2.0 * sigma_next / half_width * (operator(current) - middle_point * current)
        - sigma_now * sigma_next * previous
    )
    previous, current, sigma_now = (current, following, sigma_next)
    return current


def plane_part(center):
    span = center.shape[-1]
    margin = 2 * NZ
    padded = jnp.pad(center, ((0, 0), (0, 0), (margin, margin)))
    z_pos = jnp.arange(span, dtype=jnp.int32) % NZ

    def moved(offset):
        return lax.slice_in_dim(padded, margin + offset, margin + offset + span, axis=2)

    def z_term(offset):
        inside = ((z_pos + offset >= 0) & (z_pos + offset < NZ)).astype(jnp.float32)
        return moved(offset) * inside

    along_z = (
        -2.5 * center + 4.0 / 3.0 * (z_term(1) + z_term(-1)) - 1.0 / 12.0 * (z_term(2) + z_term(-2))
    )
    along_y = (
        -2.5 * center
        + 4.0 / 3.0 * (moved(NZ) + moved(-NZ))
        - 1.0 / 12.0 * (moved(2 * NZ) + moved(-2 * NZ))
    )
    return -0.5 * (along_y + along_z)


def energy(center, plus_one, minus_one, plus_two, minus_two, local_pot):
    along_x = -0.5 * (
        -2.5 * center + 4.0 / 3.0 * (plus_one + minus_one) - 1.0 / 12.0 * (plus_two + minus_two)
    )
    return local_pot * center + along_x + plane_part(center)


def on_device(orbitals, potential, plan, owners):
    band_width = orbitals.shape[0]
    group_count = lax.axis_size("band")
    planes = orbitals.shape[1] // group_count
    norm_factor = 1.0 / math.sqrt(orbitals.shape[1] * orbitals.shape[2])

    def whole_apply(values):
        length = values.shape[1]
        padded = jnp.pad(values, ((0, 0), (2, 2), (0, 0)))
        return energy(
            values,
            padded[:, 3 : 3 + length],
            padded[:, 1 : 1 + length],
            padded[:, 4 : 4 + length],
            padded[:, 0:length],
            potential,
        )

    filtered = chebyshev_filter(orbitals.astype(jnp.float32), whole_apply).astype(jnp.bfloat16)
    slab_orbitals = lax.all_to_all(filtered, "band", split_axis=1, concat_axis=0, tiled=True)
    padded = with_halo(slab_orbitals, (("band", 1),), 2).astype(jnp.float32)
    slab_pot = lax.dynamic_slice_in_dim(potential, lax.axis_index("band") * planes, planes, 0)
    slab_applied = energy(
        padded[:, 2 : 2 + planes],
        padded[:, 3 : 3 + planes],
        padded[:, 1 : 1 + planes],
        padded[:, 4 : 4 + planes],
        padded[:, 0:planes],
        slab_pot,
    ).astype(jnp.bfloat16)
    orbital_groups = slab_orbitals.reshape(group_count, band_width, -1)
    applied_groups = slab_applied.reshape(group_count, band_width, -1)
    collected = []
    for round_index in range(ROUNDS):
        inverse = jnp.argsort(owners[round_index])
        partner = plan[round_index]
        left_block = jnp.take(orbital_groups, inverse, axis=0)
        right_block = jnp.take(applied_groups, jnp.take(partner, inverse), axis=0)
        product = jnp.einsum(
            "kac,kbc->kab", left_block, right_block, preferred_element_type=jnp.float32
        )
        collected.append(
            lax.psum_scatter(
                (product * norm_factor).reshape(band_width * lax.axis_size("band"), band_width),
                "band",
                scatter_dimension=0,
                tiled=True,
            )
        )
    tiles = jnp.stack(collected)
    return (filtered, tiles)


def solution(mesh):
    placed = (
        P(("groups", "band"), None, None),
        P("groups", None),
        P("groups", None),
        P("groups", None),
    )
    return jax.shard_map(
        on_device,
        mesh=mesh,
        in_specs=placed,
        out_specs=(P(("groups", "band"), None, None), P(None, ("groups", "band"), None)),
        check_vma=False,
    )
```

profile of v0, /device:TPU:0, one launch (start us, length us, event | category | flops | bytes accessed | tf_op | source)
XLA Modules:
  0.0 194.6 jit_solution(11361527517866755214)
XLA Ops:
  7.2 1.3 copy_convert_fusion
  8.5 2.9 %broadcast_multiply_fusion = (f32[80,32,128]{2,0,1:T(8,128)S(1)}, f32[80,32,128]{2,0,1:T(8,128)S(1)}) fusion(f32[80,32,128]{2,0,1:T(8,128)S(1)} %copy_convert_fusion, f32[128]{0:T(128)S(1)} %get-tuple-element.22, f32[128]{0:T(128)S(1)} %get-tuple-element.23, f32[128]{0:T(128)S(1)} %get-tuple-element.24, f32[128]{0:T(128)S(1)} %get-tuple-element.25, ...), kind=kLoop, calls=%fused_computation.134 | loop fusion | flops 10485760 | bytes 3950592 | tf_op jit(solution)/shard_map/mul | solution.py:32
  11.5 3.7 %fusion.20 = bf16[80,32,128]{2,0,1:T(8,128)(2,1)} fusion(f32[80,32,128]{2,0,1:T(8,128)S(1)} %get-tuple-element.16, f32[80,32,128]{2,0,1:T(8,128)S(1)} %get-tuple-element.17, f32[32,128]{1,0:T(8,128)S(1)} %broadcast_multiply_fusion.1, f32[128]{0:T(128)S(1)} %get-tuple-element.22, f32[128]{0:T(128)S(1)} %get-tuple-element.23, f32[128]{0:T(128)S(1)} %get-tuple-element.24, ...), kind=kLoop, calls=%fused_computation.59 | loop fusion | flops 11796480 | bytes 3950592 | tf_op jit(solution)/shard_map/convert_element_type | solution.py:92
  15.2 7.5 %all-to-all-start = ((bf16[80,32,128]{2,0,1:T(8,128)(2,1)}), bf16[80,32,128]{2,0,1:T(8,128)(2,1)S(1)}, u32[]{:S(2)}, u32[]{:S(2)}) async-start(bf16[80,32,128]{2,0,1:T(8,128)(2,1)} %fusion.20), calls=%async_computation | async-start | bytes 1310720 | tf_op jit(solution)/shard_map/all_to_all | solution.py:93
  22.8 1.2 sort.31
  24.1 0.7 gather_fusion.1
  24.8 1.3 sort.32
  26.0 13.3 %all-to-all-done = bf16[80,32,128]{2,0,1:T(8,128)(2,1)S(1)} async-done(((bf16[80,32,128]{2,0,1:T(8,128)(2,1)}), bf16[80,32,128]{2,0,1:T(8,128)(2,1)S(1)}, u32[]{:S(2)}, u32[]{:S(2)}) %all-to-all-start) | async-done | bytes 655392 | tf_op jit(solution)/shard_map/all_to_all | solution.py:93
  39.3 2.1 %collective-permute-start = (bf16[1280,2,128]{2,0,1:T(8,128)(2,1)S(1)}, bf16[1280,2,128]{2,0,1:T(8,128)(2,1)S(1)}, u32[]{:S(2)}, u32[]{:S(2)}) collective-permute-start(bf16[1280,2,128]{2,0,1:T(8,128)(2,1)S(1)} %bitcast.24), channel_id=1, source_target_pairs={{0,1},{1,2},{2,3},{3,4},{4,5},{5,6},{6,7},{7,8},{8,9},{9,10},{10,1... | collective-permute-start | bytes 1966088 | tf_op jit(solution)/shard_map/ppermute | solution.py:23
  41.5 1.3 collective-permute-start.1
  43.0 0.6 gather_fusion
  43.6 2.1 %collective-permute-done.1 = bf16[1280,2,128]{2,0,1:T(8,128)(2,1)} collective-permute-done((bf16[1280,2,128]{2,0,1:T(8,128)(2,1)S(1)}, bf16[1280,2,128]{2,0,1:T(8,128)(2,1)}, u32[]{:S(2)}, u32[]{:S(2)}) %collective-permute-start.1) | collective-permute-done | bytes 655392 | tf_op jit(solution)/shard_map/ppermute | solution.py:24
  45.6 1.4 maximum_convert_fusion
  47.1 2.9 %fusion.66 = bf16[1280,2,128]{2,0,1:T(8,128)(2,1)S(1)} fusion(f32[1280,2,128]{2,0,1:T(8,128)S(1)} %slice.176, f32[1280,6,128]{2,0,1:T(8,128)S(1)} %maximum_convert_fusion, f32[128]{0:T(128)S(1)} %get-tuple-element.22, f32[128]{0:T(128)S(1)} %get-tuple-element.23, f32[128]{0:T(128)S(1)} %get-tuple-element.24, f32[128]{0:T(128)S(1)} %get-tuple-element.25, ...), kind=kLoop, calls=%fused_computation.105 | loop fusion | flops 9830400 | bytes 7212032 | tf_op jit(solution)/shard_map/convert_element_type | solution.py:103
  50.0 5.4 %copy.10 = bf16[1280,2,128]{2,1,0:T(2,128)(2,1)S(1)} copy(bf16[1280,2,128]{2,0,1:T(8,128)(2,1)S(1)} %fusion.66) | data formatting | bytes 1310720 | tf_op jit(solution)/shard_map/convert_element_type | solution.py:103
  55.9 0.6 gather_fusion.2
  56.5 1.3 convolution_multiply_fusion.1
  57.8 0.7 gather_fusion.4
  58.5 0.6 gather_fusion.3
  59.7 1.3 convolution_multiply_fusion
  61.0 2.1 %copy.11 = bf16[80,32,128]{2,1,0:T(8,128)(2,1)} copy(bf16[80,32,128]{2,0,1:T(8,128)(2,1)} %fusion.20) | data formatting | bytes 1310720
  63.1 64.1 %reduce-scatter.3.cloned.1.call-done = f32[80,80]{1,0:T(8,128)} async-done(((f32[1280,80]{1,0:T(8,128)}), f32[80,80]{1,0:T(8,128)}) %reduce-scatter.3.cloned.1.call-update) | async-done | bytes 25616 | tf_op jit(solution)/shard_map/reduce_scatter | solution.py:116
  127.2 59.1 %reduce-scatter.5.cloned.1.call-done = f32[80,80]{1,0:T(8,128)} async-done(((f32[1280,80]{1,0:T(8,128)}), f32[80,80]{1,0:T(8,128)}) %reduce-scatter.5.cloned.1.call-update) | async-done | bytes 25616 | tf_op jit(solution)/shard_map/reduce_scatter | solution.py:116
  186.3 1.4 pad_maximum_fusion
  (34 shorter events, 1.5 us)
Async XLA Ops:
  7.2 1.3 copy-start.1
  8.5 2.9 %copy-start = (bf16[80,32,128]{2,1,0:T(8,128)(2,1)S(1)}, bf16[80,32,128]{2,1,0:T(8,128)(2,1)}, u32[]{:S(2)}) copy-start(bf16[80,32,128]{2,1,0:T(8,128)(2,1)} %param.8) | copy-start | bytes 1966084
  15.2 7.6 %copy-start.2 = (s32[2,16]{1,0:T(2,128)S(1)}, s32[2,16]{1,0:T(2,128)}, u32[]{:S(2)}) copy-start(s32[2,16]{1,0:T(2,128)} %param.11) | copy-start | bytes 388
  15.2 8.9 %copy-start.3 = (s32[2,16]{1,0:T(2,128)S(1)}, s32[2,16]{1,0:T(2,128)}, u32[]{:S(2)}) copy-start(s32[2,16]{1,0:T(2,128)} %param.10) | copy-start | bytes 388
  15.2 24.1 %all-to-all-start = ((bf16[80,32,128]{2,0,1:T(8,128)(2,1)}), bf16[80,32,128]{2,0,1:T(8,128)(2,1)S(1)}, u32[]{:S(2)}, u32[]{:S(2)}) async-start(bf16[80,32,128]{2,0,1:T(8,128)(2,1)} %fusion.20), calls=%async_computation | async-start | bytes 1310720 | tf_op jit(solution)/shard_map/all_to_all | solution.py:93
  22.7 104.5 %reduce-scatter.3.cloned.1.call-start = ((), (), s32[]{:S(2)}) async-start(), calls=%async_computation.3 | async-start | bytes 696320 | tf_op jit(solution)/shard_map/reduce_scatter | solution.py:116
  39.3 4.2 %collective-permute-start = (bf16[1280,2,128]{2,0,1:T(8,128)(2,1)S(1)}, bf16[1280,2,128]{2,0,1:T(8,128)(2,1)S(1)}, u32[]{:S(2)}, u32[]{:S(2)}) collective-permute-start(bf16[1280,2,128]{2,0,1:T(8,128)(2,1)S(1)} %bitcast.24), channel_id=1, source_target_pairs={{0,1},{1,2},{2,3},{3,4},{4,5},{5,6},{6,7},{7,8},{8,9},{9,10},{10,1... | collective-permute-start | bytes 1966088 | tf_op jit(solution)/shard_map/ppermute | solution.py:23
  41.5 4.2 %collective-permute-start.1 = (bf16[1280,2,128]{2,0,1:T(8,128)(2,1)S(1)}, bf16[1280,2,128]{2,0,1:T(8,128)(2,1)}, u32[]{:S(2)}, u32[]{:S(2)}) collective-permute-start(bf16[1280,2,128]{2,0,1:T(8,128)(2,1)S(1)} %bitcast.25), channel_id=1, source_target_pairs={{1,0},{2,1},{3,2},{4,3},{5,4},{6,5},{7,6},{8,7},{9,8},{10,9},{11,1... | collective-permute-start | bytes 1966088 | tf_op jit(solution)/shard_map/ppermute | solution.py:24
  57.8 128.6 %reduce-scatter.5.cloned.1.call-start = ((), (), s32[]{:S(2)}) async-start(), calls=%async_computation.4 | async-start | bytes 696320 | tf_op jit(solution)/shard_map/reduce_scatter | solution.py:116
Sparse Core Ops, SparseCore 0:
  57.9 69.2 reduce-scatter.2
  130.7 55.5 reduce-scatter.4
where the time goes:
time: 195 us
  waiting for transfers between devices  139 us (71%)
  other arithmetic  16.2 us (8%)
  between operations  14.3 us (7%)
  local copies, waits for them, and re-layouts  11.9 us (6%)
  starting transfers between devices  11 us (6%)
  matrix products  2.55 us (1%)
    reduce_scatter x2, waiting for transfers between devices, on_device(): lax.psum_scatter((product * norm_factor).reshape(band_width * lax.axis_si...  123 us
    all_to_all x1, waiting for transfers between devices, on_device(): lax.all_to_all(filtered, 'band', split_axis=1, concat_axis=0, tiled=True)  13.3 us
    all_to_all x1, starting transfers between devices, on_device(): lax.all_to_all(filtered, 'band', split_axis=1, concat_axis=0, tiled=True)  7.55 us
    convert_element_type x1, local copies, waits for them, and re-layouts, on_device(): slab_applied = energy(padded[:, 2:2 + planes], padded[:, 3:3 + planes], p...  5.44 us
  transfers between devices with their start and end apart: 5, of which 4 were waited for; matrix products, arithmetic and copies ran while one was open for 5% of the time, Pallas kernels for 0%

commit v1 on v0

--- a/solution.py
+++ b/solution.py
@@ -90,7 +90,10 @@
         )
 
     filtered = chebyshev_filter(orbitals.astype(jnp.float32), whole_apply).astype(jnp.bfloat16)
-    slab_orbitals = lax.all_to_all(filtered, "band", split_axis=1, concat_axis=0, tiled=True)
+    slab_orbitals = jnp.concatenate(
+        lax.all_to_all(jnp.stack(jnp.split(filtered, lax.axis_size("band"), axis=1)), "band", 0, 0),
+        axis=0,
+    )
     padded = with_halo(slab_orbitals, (("band", 1),), 2).astype(jnp.float32)
     slab_pot = lax.dynamic_slice_in_dim(potential, lax.axis_index("band") * planes, planes, 0)
     slab_applied = energy(

time: 195 us -> 205 us (1.051)
  local copies, waits for them, and re-layouts: 11.9 us -> 20.6 us
    unnamed x9 -> x25, local copies, waits for them, and re-layouts: 2.11 us -> 9.8 us
    reduce_scatter x2, waiting for transfers between devices: 123 us -> 126 us  [on_device(): lax.psum_scatter((product * norm_factor).reshape(band_width * lax.axis_si...]
  transfers between devices with their start and end apart: 5 -> 5, of which waited for: 4 -> 4; matrix products, arithmetic and copies ran while one was open for 5% -> 4% of each run, Pallas kernels for 0% -> 0%
where the time goes in v1:
time: 205 us; the launch traced here: 204 us
  waiting for transfers between devices  140 us (68%)
  local copies, waits for them, and re-layouts  20.6 us (10%)
  other arithmetic  15.4 us (8%)
  between operations  14.3 us (7%)
  starting transfers between devices  10.9 us (5%)
  matrix products  2.52 us (1%)
    reduce_scatter x2, waiting for transfers between devices, on_device(): lax.psum_scatter((product * norm_factor).reshape(band_width * lax.axis_si...  126 us
    all_to_all x1, waiting for transfers between devices, on_device(): lax.all_to_all(jnp.stack(jnp.split(filtered, lax.axis_size('band'), axis=...  12.6 us
    unnamed x25, local copies, waits for them, and re-layouts  9.8 us
    all_to_all x1, starting transfers between devices, on_device(): lax.all_to_all(jnp.stack(jnp.split(filtered, lax.axis_size('band'), axis=...  7.41 us
    convert_element_type x1, local copies, waits for them, and re-layouts, on_device(): slab_applied = energy(padded[:, 2:2 + planes], padded[:, 3:3 + planes], p...  5.44 us
  transfers between devices with their start and end apart: 5, of which 4 were waited for; matrix products, arithmetic and copies ran while one was open for 4% of the time, Pallas kernels for 0%

profile of v1, /device:TPU:0, one launch (start us, length us, event | category | flops | bytes accessed | tf_op | source)
XLA Modules:
  0.0 204.2 jit_solution(12963302146448391239)
XLA Ops:
  7.2 1.2 convert_element_type.72
  8.5 2.9 %broadcast_multiply_fusion = (f32[80,32,128]{2,1,0:T(8,128)S(1)}, f32[80,32,128]{2,1,0:T(8,128)S(1)}) fusion(f32[80,32,128]{2,1,0:T(8,128)S(1)} %convert_element_type.72, f32[128]{0:T(128)S(1)} %get-tuple-element.20, f32[128]{0:T(128)S(1)} %get-tuple-element.21, f32[128]{0:T(128)S(1)} %get-tuple-element.22, f32[128]{0:T(128)S(1)} %get-tuple-element.23, ...), kind=kLoop, calls=%fused_computation.132 | loop fusion | flops 10485760 | bytes 3950592 | tf_op jit(solution)/shard_map/mul | solution.py:32
  11.4 2.9 %fusion.20 = bf16[80,32,128]{2,1,0:T(8,128)(2,1)S(1)} fusion(f32[80,32,128]{2,1,0:T(8,128)S(1)} %get-tuple-element.14, f32[80,32,128]{2,1,0:T(8,128)S(1)} %get-tuple-element.15, f32[32,128]{1,0:T(8,128)S(1)} %broadcast_multiply_fusion.1, f32[128]{0:T(128)S(1)} %get-tuple-element.20, f32[128]{0:T(128)S(1)} %get-tuple-element.21, ...), kind=kLoop, calls=%fused_computation.59 | loop fusion | flops 11796480 | bytes 3950592 | tf_op jit(solution)/shard_map/convert_element_type | solution.py:92
  17.6 0.7 fusion.105
  18.9 0.7 fusion.103
  20.2 0.7 fusion.101
  22.8 0.7 fusion.97
  23.5 0.7 fusion.96
  24.8 7.4 %all-to-all-start = ((bf16[16,80,2,128]{3,2,1,0:T(2,128)(2,1)}), bf16[16,80,2,128]{3,2,1,0:T(2,128)(2,1)S(1)}, u32[]{:S(2)}, u32[]{:S(2)}) async-start(bf16[16,80,2,128]{3,2,1,0:T(2,128)(2,1)} %fusion.95), calls=%async_computation | async-start | bytes 1310720 | tf_op jit(solution)/shard_map/all_to_all | solution.py:94
  32.3 1.2 sort.32
  33.6 0.7 gather_fusion.4
  34.3 1.3 sort.31
  36.2 12.6 %all-to-all-done = bf16[16,80,2,128]{3,2,1,0:T(2,128)(2,1)S(1)} async-done(((bf16[16,80,2,128]{3,2,1,0:T(2,128)(2,1)}), bf16[16,80,2,128]{3,2,1,0:T(2,128)(2,1)S(1)}, u32[]{:S(2)}, u32[]{:S(2)}) %all-to-all-start) | async-done | bytes 655392 | tf_op jit(solution)/shard_map/all_to_all | solution.py:94
  48.9 2.1 %collective-permute-start = (bf16[1280,2,128]{2,0,1:T(8,128)(2,1)S(1)}, bf16[1280,2,128]{2,0,1:T(8,128)(2,1)S(1)}, u32[]{:S(2)}, u32[]{:S(2)}) collective-permute-start(bf16[1280,2,128]{2,0,1:T(8,128)(2,1)S(1)} %bitcast.77), channel_id=1, source_target_pairs={{0,1},{1,2},{2,3},{3,4},{4,5},{5,6},{6,7},{7,8},{8,9},{9,10},{10,1... | collective-permute-start | bytes 1966088 | tf_op jit(solution)/shard_map/ppermute | solution.py:23
  51.0 1.3 collective-permute-start.1
  53.4 1.8 collective-permute-done.1
  55.2 1.4 maximum_convert_fusion
  56.7 2.9 %fusion.66 = bf16[1280,2,128]{2,0,1:T(8,128)(2,1)S(1)} fusion(f32[1280,2,128]{2,0,1:T(8,128)S(1)} %slice.176, f32[1280,6,128]{2,0,1:T(8,128)S(1)} %maximum_convert_fusion, f32[128]{0:T(128)S(1)} %get-tuple-element.20, f32[128]{0:T(128)S(1)} %get-tuple-element.21, f32[128]{0:T(128)S(1)} %get-tuple-element.22, f32[128]{0:T(128)S(1)} %get-tuple-element.23, ...), kind=kLoop, calls=%fused_computation.105 | loop fusion | flops 9830400 | bytes 7212032 | tf_op jit(solution)/shard_map/convert_element_type | solution.py:106
  59.6 5.4 %copy.8 = bf16[1280,2,128]{2,1,0:T(2,128)(2,1)S(1)} copy(bf16[1280,2,128]{2,0,1:T(8,128)(2,1)S(1)} %fusion.66) | data formatting | bytes 1310720 | tf_op jit(solution)/shard_map/convert_element_type | solution.py:106
  66.0 1.3 convolution_multiply_fusion.1
  68.6 1.3 convolution_multiply_fusion
  69.9 66.9 %reduce-scatter.3.cloned.1.call-done = f32[80,80]{1,0:T(8,128)} async-done(((f32[1280,80]{1,0:T(8,128)}), f32[80,80]{1,0:T(8,128)}) %reduce-scatter.3.cloned.1.call-update) | async-done | bytes 25616 | tf_op jit(solution)/shard_map/reduce_scatter | solution.py:119
  136.7 59.1 %reduce-scatter.5.cloned.1.call-done = f32[80,80]{1,0:T(8,128)} async-done(((f32[1280,80]{1,0:T(8,128)}), f32[80,80]{1,0:T(8,128)}) %reduce-scatter.5.cloned.1.call-update) | async-done | bytes 25616 | tf_op jit(solution)/shard_map/reduce_scatter | solution.py:119
  195.9 1.4 pad_maximum_fusion
  (50 shorter events, 11.4 us)
Async XLA Ops:
  7.2 1.3 copy-start.2
  8.5 2.9 %copy-start = (bf16[80,32,128]{2,1,0:T(8,128)(2,1)S(1)}, bf16[80,32,128]{2,1,0:T(8,128)(2,1)}, u32[]{:S(2)}) copy-start(bf16[80,32,128]{2,1,0:T(8,128)(2,1)} %param.8) | copy-start | bytes 1966084
  14.3 10.5 %copy-start.1 = (bf16[80,32,128]{2,1,0:T(8,128)(2,1)}, bf16[80,32,128]{2,1,0:T(8,128)(2,1)S(1)}, u32[]{:S(2)}) copy-start(bf16[80,32,128]{2,1,0:T(8,128)(2,1)S(1)} %fusion.20) | copy-start | bytes 1966084
  14.4 17.9 %copy-start.3 = (s32[2,16]{1,0:T(2,128)S(1)}, s32[2,16]{1,0:T(2,128)}, u32[]{:S(2)}) copy-start(s32[2,16]{1,0:T(2,128)} %param.11) | copy-start | bytes 388
  14.4 19.2 %copy-start.4 = (s32[2,16]{1,0:T(2,128)S(1)}, s32[2,16]{1,0:T(2,128)}, u32[]{:S(2)}) copy-start(s32[2,16]{1,0:T(2,128)} %param.10) | copy-start | bytes 388
  24.8 24.0 %all-to-all-start = ((bf16[16,80,2,128]{3,2,1,0:T(2,128)(2,1)}), bf16[16,80,2,128]{3,2,1,0:T(2,128)(2,1)S(1)}, u32[]{:S(2)}, u32[]{:S(2)}) async-start(bf16[16,80,2,128]{3,2,1,0:T(2,128)(2,1)} %fusion.95), calls=%async_computation | async-start | bytes 1310720 | tf_op jit(solution)/shard_map/all_to_all | solution.py:94
  32.2 104.5 %reduce-scatter.3.cloned.1.call-start = ((), (), s32[]{:S(2)}) async-start(), calls=%async_computation.3 | async-start | bytes 696320 | tf_op jit(solution)/shard_map/reduce_scatter | solution.py:119
  48.9 4.5 %collective-permute-start = (bf16[1280,2,128]{2,0,1:T(8,128)(2,1)S(1)}, bf16[1280,2,128]{2,0,1:T(8,128)(2,1)S(1)}, u32[]{:S(2)}, u32[]{:S(2)}) collective-permute-start(bf16[1280,2,128]{2,0,1:T(8,128)(2,1)S(1)} %bitcast.77), channel_id=1, source_target_pairs={{0,1},{1,2},{2,3},{3,4},{4,5},{5,6},{6,7},{7,8},{8,9},{9,10},{10,1... | collective-permute-start | bytes 1966088 | tf_op jit(solution)/shard_map/ppermute | solution.py:23
  51.0 4.2 %collective-permute-start.1 = (bf16[1280,2,128]{2,0,1:T(8,128)(2,1)S(1)}, bf16[1280,2,128]{2,0,1:T(8,128)(2,1)}, u32[]{:S(2)}, u32[]{:S(2)}) collective-permute-start(bf16[1280,2,128]{2,0,1:T(8,128)(2,1)S(1)} %bitcast.78), channel_id=1, source_target_pairs={{1,0},{2,1},{3,2},{4,3},{5,4},{6,5},{7,6},{8,7},{9,8},{10,9},{11,1... | collective-permute-start | bytes 1966088 | tf_op jit(solution)/shard_map/ppermute | solution.py:24
  67.3 128.6 %reduce-scatter.5.cloned.1.call-start = ((), (), s32[]{:S(2)}) async-start(), calls=%async_computation.4 | async-start | bytes 696320 | tf_op jit(solution)/shard_map/reduce_scatter | solution.py:119
Sparse Core Ops, SparseCore 0:
  67.4 69.2 reduce-scatter.2
  140.3 55.5 reduce-scatter.4
